TPU v7x, 512 devices: a whole 4x8x8 slice. The times are simulated.
512 devices in a mesh: sector: 64 (over y, z), term: 8 (over x, core).
Axes of the slice: x: 4, y: 8, z: 8, core: 2. Of those that a mesh axis runs over, the one named last changes fastest.
Arguments:
- psi: bfloat16 [4, 64, 4, 256, 256], P(None, 'sector'), may hold values from -6 to 6
- left_env: bfloat16 [16, 64, 256, 256], P('term', 'sector'), may hold values from -0.375 to 0.375
- right_env: bfloat16 [16, 64, 256, 256], P('term', 'sector'), may hold values from -0.375 to 0.375
- op_index: int32 [16], P('term'), may hold values from 0 to 4
- kept_rows: int32 [64], P('sector'), may hold values from 64 to 256, as said below
Outputs:
- sigma: float32 [4, 64, 4, 256, 256], P(None, 'sector', None, 'term')
Inputs may be any that keep to these rules, and one draw needn't show every extreme that they name: `kept_rows`: some sector keeps all 256 rows and some other keeps 256 // 4.
All inputs are finite; a program needn't handle non-finite values.
Results may differ from a plain program's by a relative error of at most 0.0029.
Values may be sent and summed in bfloat16 or wider, within the bound.
A program may use at most 64 MiB of HBM per device.

v0:
```python
import jax
import jax.numpy as jnp
from jax import lax
from jax.sharding import PartitionSpec as P

OP_KINDS = 5


def padded_2(block, sides, width):
    for axis, dim in sides:
        count = lax.axis_size(axis)
        forward = [(i, i + 1) for i in range(count - 1)]
        backward = [(target, source) for source, target in forward]
        low = lax.ppermute(
            lax.slice_in_dim(block, block.shape[dim] - width, None, axis=dim), axis, forward
        )
        high = lax.ppermute(lax.slice_in_dim(block, 0, width, axis=dim), axis, backward)
        block = jnp.concatenate([low, block, high], axis=dim)
    return block


def diagonal_matrix(values):
    return [[values[r] if r == c else 0.0 for c in range(4)] for r in range(4)]


def operator_table():
    flip = [[0.0, 0.0, 0.0, 0.0], [0.0, 0.0, 0.5, 0.0], [0.0, 0.5, 0.0, 0.0], [0.0, 0.0, 0.0, 0.0]]
    stacked = [
        diagonal_matrix([1.0, 1.0, 1.0, 1.0]),
        diagonal_matrix([0.25, -0.25, -0.25, 0.25]),
        flip,
        diagonal_matrix([0.5, 0.5, -0.5, -0.5]),
        diagonal_matrix([0.5, -0.5, 0.5, -0.5]),
    ]
    return jnp.asarray(stacked, jnp.float32)


def combine_terms(term_factor, mapped_vectors):
    return jnp.einsum(
        "uci,ufimy->fcmy", term_factor, mapped_vectors, precision=lax.Precision.HIGHEST
    )


def finish_sum(blocks_full, own_rows):
    row_ids = jnp.arange(blocks_full.shape[2], dtype=jnp.int32)
    blocks_full = jnp.where(row_ids[None, None, :, None] < own_rows, blocks_full, 0.0)
    return lax.psum_scatter(blocks_full, "term", scatter_dimension=2, tiled=True)


def shards(psi, left_env, right_env, op_index, kept_rows):
    trial_vectors = psi[:, 0]
    left_mat = left_env[:, 0]
    right_mat = right_env[:, 0]
    size_b = trial_vectors.shape[-1]
    onehot = (op_index[:, None] == jnp.arange(OP_KINDS, dtype=jnp.int32)[None, :]).astype(
        jnp.float32
    )
    term_factor = jnp.einsum(
        "tk,kpq->tpq", onehot, operator_table(), precision=lax.Precision.HIGHEST
    )
    lifted = jnp.einsum(
        "tab,vpbc->tvpac", left_mat, trial_vectors, preferred_element_type=jnp.float32
    ).astype(jnp.bfloat16)
    own_rows = kept_rows[0]
    indices = jnp.arange(size_b, dtype=jnp.int32)
    rim_blocks = jnp.stack([lifted[:, :, 3], lifted[:, :, 0]], 0)
    padded = padded_2(rim_blocks, (("sector", 0),), 1)
    arrived = jnp.stack([padded[0], lifted[:, :, 1], lifted[:, :, 2], padded[3]], 2)
    mapped_vectors = jnp.einsum(
        "tvpac,tdc->tvpad", arrived, right_mat, preferred_element_type=jnp.float32
    )
    right_side = combine_terms(term_factor, mapped_vectors)
    right_side = jnp.where(indices[None, None, None, :] < own_rows, right_side, 0.0)
    returned = padded_2(jnp.stack([right_side[:, 0], right_side[:, 3]], 0), (("sector", 0),), 1)
    blocks_full = jnp.stack([returned[3], right_side[:, 1], right_side[:, 2], returned[0]], 1)
    result = finish_sum(blocks_full, own_rows)
    return result[:, None]


def solution(mesh):
    in_specs = (
        P(None, "sector", None, None, None),
        P("term", "sector", None, None),
        P("term", "sector", None, None),
        P("term"),
        P("sector"),
    )
    out_specs = P(None, "sector", None, "term", None)
    return jax.shard_map(shards, mesh=mesh, in_specs=in_specs, out_specs=out_specs, check_vma=False)
```

profile of v0, /device:TPU:1, one launch (start us, length us, event | category | flops | bytes accessed | tf_op | source)
XLA Modules:
  0.0 159.6 jit_solution(8894938351564778551)
XLA Ops:
  6.5 0.0 copy-start
  6.5 0.0 reduce-scatter.5.cloned.1.call-start
  6.5 1.6 copy-done
  8.1 2.3 %convert_bitcast_fusion = bf16[2,4,4,256,256]{3,4,0,2,1:T(8,128)(2,1)S(1)} fusion(bf16[4,1,4,256,256]{4,3,2,1,0:T(8,128)(2,1)S(1)} %copy-done, bf16[2,1,256,256]{3,2,1,0:T(8,128)(2,1)} %param.7), kind=kOutput, calls=%fused_computation.9 | convolution fusion | flops 1075838976 | bytes 6553600 | tf_op jit(solution)/shard_map/tab,vpbc->tvpac/dot_general | solution.py:61
  10.4 0.0 copy-start.2
  10.4 0.0 copy-start.3
  10.4 0.0 copy-start.1
  10.4 0.1 slice_bitcast_fusion.3
  10.6 4.9 %collective-permute-start = (bf16[1,2,4,256,256]{3,4,1,2,0:T(8,128)(2,1)S(1)}, bf16[1,2,4,256,256]{3,4,1,2,0:T(8,128)(2,1)S(1)}, u32[]{:S(2)}, u32[]{:S(2)}) collective-permute-start(bf16[1,2,4,256,256]{3,4,1,2,0:T(8,128)(2,1)S(1)} %get-tuple-element.7), channel_id=1, source_target_pairs={{0,8},{8,16},{16,24},{24,32},{32,40},{40,48},{48,56},{56,64},{64,7... | collective-permute-start | bytes 3145736 | tf_op jit(solution)/shard_map/ppermute | solution.py:14
  15.5 1.3 collective-permute-start.1
  16.8 0.2 slice.29
  17.6 0.0 copy-done.2
  17.6 0.0 copy-done.3
  17.6 0.2 convolution_bitcast_fusion
  17.9 17.0 %collective-permute-done = bf16[1,2,4,256,256]{3,4,1,2,0:T(8,128)(2,1)S(1)} collective-permute-done((bf16[1,2,4,256,256]{3,4,1,2,0:T(8,128)(2,1)S(1)}, bf16[1,2,4,256,256]{3,4,1,2,0:T(8,128)(2,1)S(1)}, u32[]{:S(2)}, u32[]{:S(2)}) %collective-permute-start) | collective-permute-done | bytes 1048608 | tf_op jit(solution)/shard_map/ppermute | solution.py:14
  34.9 5.1 %collective-permute-done.1 = bf16[1,2,4,256,256]{3,4,1,2,0:T(8,128)(2,1)S(1)} collective-permute-done((bf16[1,2,4,256,256]{3,4,1,2,0:T(8,128)(2,1)S(1)}, bf16[1,2,4,256,256]{3,4,1,2,0:T(8,128)(2,1)S(1)}, u32[]{:S(2)}, u32[]{:S(2)}) %collective-permute-start.1) | collective-permute-done | bytes 1048608 | tf_op jit(solution)/shard_map/ppermute | solution.py:17
  39.9 0.0 copy-done.1
  39.9 2.3 %fusion.3 = f32[2,4,4,256,256]{4,3,2,1,0:T(8,128)S(1)} fusion(bf16[2,1,256,256]{3,2,1,0:T(8,128)(2,1)S(1)} %copy-done.1, bf16[2,4,1,256,256]{3,4,0,2,1:T(8,128)(2,1)S(1)} %bitcast.67, bf16[2,4,2,256,256]{3,4,0,2,1:T(8,128)(2,1)S(1)} %slice.29, bf16[2,4,1,256,256]{3,4,0,2,1:T(8,128)(2,1)S(1)} %bitcast.66), kind=kOutput, calls=%fused_computation.7 | convolution fusion | flops 1077936128 | bytes 12845056 | tf_op jit(solution)/shard_map/tvpac,tdc->tvpad/dot_general | solution.py:69
  42.2 14.2 %fusion.2 = f32[4,4,256,256]{3,1,2,0:T(4,128)S(1)} fusion(f32[2,4,4,256,256]{4,3,2,1,0:T(8,128)S(1)} %fusion.3, pred[256]{0:T(512)(128)(4,1)S(1)} %iota_compare_fusion, f32[2,4,4,1,1]{2,0,1,4,3:T(2,128)S(1)} %convolution_bitcast_fusion), kind=kOutput, calls=%fused_computation.6 | convolution fusion | flops 101711872 | bytes 12583296 | tf_op jit(solution)/shard_map/uci,ufimy->fcmy/dot_general | solution.py:39
  56.4 1.6 %slice_bitcast_fusion.1 = (f32[1,4,256,256]{3,0,2,1:T(1,128)S(1)}, f32[1,4,256,256]{3,0,2,1:T(1,128)S(1)}) fusion(f32[4,4,256,256]{3,1,2,0:T(4,128)S(1)} %fusion.2), kind=kLoop, calls=%fused_computation.13 | loop fusion | bytes 4194304 | tf_op jit(solution)/shard_map/stack;squeeze | solution.py:74
  58.0 1.3 collective-permute-start.2
  59.3 6.9 %collective-permute-start.3 = (f32[1,4,256,256]{3,0,2,1:T(1,128)S(1)}, f32[1,4,256,256]{3,0,2,1:T(1,128)S(1)}, u32[]{:S(2)}, u32[]{:S(2)}) collective-permute-start(f32[1,4,256,256]{3,0,2,1:T(1,128)S(1)} %get-tuple-element.6), channel_id=1, source_target_pairs={{0,8},{8,16},{16,24},{24,32},{32,40},{40,48},{48,56},{56,64},{64,7... | collective-permute-start | bytes 3145736 | tf_op jit(solution)/shard_map/ppermute | solution.py:14
  66.2 1.1 slice.32
  67.3 18.7 %collective-permute-done.2 = f32[1,4,256,256]{3,0,2,1:T(1,128)S(1)} collective-permute-done((f32[1,4,256,256]{3,0,2,1:T(1,128)S(1)}, f32[1,4,256,256]{3,0,2,1:T(1,128)S(1)}, u32[]{:S(2)}, u32[]{:S(2)}) %collective-permute-start.2) | collective-permute-done | bytes 1048608 | tf_op jit(solution)/shard_map/ppermute | solution.py:17
  86.0 0.9 collective-permute-done.3
  86.9 5.7 %copy_bitcast_fusion = f32[256,4,4,256]{3,2,1,0:T(4,128)} fusion(f32[4,1,256,256]{3,1,2,0:T(1,128)S(1)} %bitcast.65, f32[4,2,256,256]{3,1,2,0:T(2,128)S(1)} %slice.32, f32[4,1,256,256]{3,1,2,0:T(1,128)S(1)} %bitcast.64, pred[256]{0:T(512)(128)(4,1)S(1)} %iota_compare_fusion), kind=kLoop, calls=%fused_computation.4 | loop fusion | flops 3145728 | bytes 8388864
  92.6 5.8 %reshape.17 = f32[256,4096]{1,0:T(8,128)} reshape(f32[256,4,4,256]{3,2,1,0:T(4,128)} %copy_bitcast_fusion) | data formatting | bytes 8388608
  98.4 0.0 reduce-scatter.5.cloned.1.call-update
  98.4 52.0 %reduce-scatter.5.cloned.1.call-done = f32[32,4096]{1,0:T(8,128)} async-done(((f32[256,4096]{1,0:T(8,128)}), f32[32,4096]{1,0:T(8,128)}) %reduce-scatter.5.cloned.1.call-update) | async-done | bytes 524304
  150.4 1.4 reshape.18
  151.9 0.9 copy.14
  (2 shorter events, 0.0 us)
Async XLA Ops:
  6.5 1.6 copy-start
  6.5 143.9 %reduce-scatter.5.cloned.1.call-start = ((), (), s32[]{:S(2)}) async-start(), calls=%async_computation.1 | async-start | bytes 4718592
  10.4 7.2 %copy-start.2 = (s32[2]{0:T(128)S(1)}, s32[2]{0:T(128)}, u32[]{:S(2)}) copy-start(s32[2]{0:T(128)} %param.9) | copy-start | bytes 28
  10.4 7.2 %copy-start.3 = (f32[5,4,4]{0,2,1:T(4,128)S(1)}, f32[5,4,4]{0,2,1:T(4,128)}, u32[]{:S(2)}) copy-start(f32[5,4,4]{0,2,1:T(4,128)} %constant.10) | copy-start | bytes 964
  10.4 29.5 %copy-start.1 = (bf16[2,1,256,256]{3,2,1,0:T(8,128)(2,1)S(1)}, bf16[2,1,256,256]{3,2,1,0:T(8,128)(2,1)}, u32[]{:S(2)}) copy-start(bf16[2,1,256,256]{3,2,1,0:T(8,128)(2,1)} %param.8) | copy-start | bytes 786436
  10.6 24.3 %collective-permute-start = (bf16[1,2,4,256,256]{3,4,1,2,0:T(8,128)(2,1)S(1)}, bf16[1,2,4,256,256]{3,4,1,2,0:T(8,128)(2,1)S(1)}, u32[]{:S(2)}, u32[]{:S(2)}) collective-permute-start(bf16[1,2,4,256,256]{3,4,1,2,0:T(8,128)(2,1)S(1)} %get-tuple-element.7), channel_id=1, source_target_pairs={{0,8},{8,16},{16,24},{24,32},{32,40},{40,48},{48,56},{56,64},{64,7... | collective-permute-start | bytes 3145736 | tf_op jit(solution)/shard_map/ppermute | solution.py:14
  15.5 24.5 %collective-permute-start.1 = (bf16[1,2,4,256,256]{3,4,1,2,0:T(8,128)(2,1)S(1)}, bf16[1,2,4,256,256]{3,4,1,2,0:T(8,128)(2,1)S(1)}, u32[]{:S(2)}, u32[]{:S(2)}) collective-permute-start(bf16[1,2,4,256,256]{3,4,1,2,0:T(8,128)(2,1)S(1)} %get-tuple-element.8), channel_id=1, source_target_pairs={{8,0},{16,8},{24,16},{32,24},{40,32},{48,40},{56,48},{64,56},{72,6... | collective-permute-start | bytes 3145736 | tf_op jit(solution)/shard_map/ppermute | solution.py:17
  58.0 28.0 %collective-permute-start.2 = (f32[1,4,256,256]{3,0,2,1:T(1,128)S(1)}, f32[1,4,256,256]{3,0,2,1:T(1,128)S(1)}, u32[]{:S(2)}, u32[]{:S(2)}) collective-permute-start(f32[1,4,256,256]{3,0,2,1:T(1,128)S(1)} %get-tuple-element.5), channel_id=1, source_target_pairs={{8,0},{16,8},{24,16},{32,24},{40,32},{48,40},{56,48},{64,56},{72,6... | collective-permute-start | bytes 3145736 | tf_op jit(solution)/shard_map/ppermute | solution.py:17
  59.3 27.6 %collective-permute-start.3 = (f32[1,4,256,256]{3,0,2,1:T(1,128)S(1)}, f32[1,4,256,256]{3,0,2,1:T(1,128)S(1)}, u32[]{:S(2)}, u32[]{:S(2)}) collective-permute-start(f32[1,4,256,256]{3,0,2,1:T(1,128)S(1)} %get-tuple-element.6), channel_id=1, source_target_pairs={{0,8},{8,16},{16,24},{24,32},{32,40},{40,48},{48,56},{56,64},{64,7... | collective-permute-start | bytes 3145736 | tf_op jit(solution)/shard_map/ppermute | solution.py:14
Sparse Core Ops, SparseCore 0:
  98.5 51.8 reduce-scatter.4
where the time goes:
time: 161 us; the launch traced here: 160 us
  waiting for transfers between devices  93.7 us (58%)
  matrix products  18.9 us (12%)
  starting transfers between devices  14.4 us (9%)
  between operations  14.2 us (9%)
  local copies, waits for them, and re-layouts  12.7 us (8%)
  other arithmetic  5.66 us (4%)
    unnamed x2, waiting for transfers between devices  52 us
    ppermute x2, waiting for transfers between devices, padded_2(): lax.ppermute(lax.slice_in_dim(block, 0, width, axis=dim), axis, backward)  23.8 us
    ppermute x2, waiting for transfers between devices, padded_2(): lax.ppermute(lax.slice_in_dim(block, block.shape[dim] - width, None, axis...  17.9 us
    dot_general x1, matrix products, combine_terms(): jnp.einsum('uci,ufimy->fcmy', term_factor, mapped_vectors, precision=lax....  14.2 us
    ppermute x2, starting transfers between devices, padded_2(): lax.ppermute(lax.slice_in_dim(block, block.shape[dim] - width, None, axis...  11.8 us
    unnamed x10, local copies, waits for them, and re-layouts  8.78 us
    unnamed x1, other arithmetic  5.65 us
  transfers between devices with their start and end apart: 5, of which 5 were waited for; matrix products, arithmetic and copies ran while one was open for 1% of the time, Pallas kernels for 0%

commit v1 on v0

v1 whole, which is shorter than its diff:
```python
import functools

import jax
import jax.numpy as jnp
from jax import lax
from jax.experimental import pallas as pl
from jax.experimental.pallas import tpu as pltpu
from jax.sharding import PartitionSpec as P

F32 = jnp.float32
BF16 = jnp.bfloat16
NX = 4


def local(src, dst, sem):
    return pltpu.make_async_copy(src, dst, sem)


def remote(src, dst, send, recv, dev):
    return pltpu.make_async_remote_copy(
        src_ref=src, dst_ref=dst, send_sem=send, recv_sem=recv, device_id=dev, device_id_type=pl.DeviceIdType.MESH
    )


def nt_dot(a, b):
    return lax.dot_general(a, b, (((1,), (1,)), ((), ())), preferred_element_type=F32)


def kernel(
    sectors, psi, left, right, op, kept, out,
    pin, pout, lraw, lin, lout, rown, rnbr, mo, mall, mz,
    sb, kf, rs, ry, rx, po, loc, ob,
    s_load, s_pl, r_pl, s_pr, r_pr, s_pm, r_pm, s_zr, r_zr, s_zm, r_zm,
    s_d2, r_ry, s_dir, s_rel, r_rx, s_po, r_po, s_out,
):
    nvec, _, size, _ = psi.shape
    rc, rd = size // NX, size // NX // 2
    s = lax.axis_index("sector")
    k = lax.axis_index("term")
    x, c = lax.div(k, 2), lax.rem(k, 2)
    up = lax.rem(s + 1, sectors)
    down = lax.rem(s + sectors - 1, sectors)
    plus = lax.rem(x + 1, NX)
    minus = lax.rem(x + NX - 1, NX)
    partner = (s, 2 * x + 1 - c)
    own2 = pl.ds(2 * c, 2)
    chips = [lax.rem(x + off, NX) for off in (2, 1, 3, 0)]
    toward = [plus, minus]

    loads = [local(left.at[:, chips[i]], lraw.at[own2, pl.ds(i * rc, rc)], s_load.at[i]) for i in range(4)]
    loads += [
        local(right, rown.at[own2], s_load.at[4]),
        local(psi.at[:, 1 + c], pin.at[:, 0], s_load.at[5]),
        local(psi.at[:, 2 - c], pin.at[:, 1], s_load.at[6]),
        local(psi.at[:, 3 * c], pout, s_load.at[7]),
    ]
    for copy in loads:
        copy.start()
    row8 = lax.broadcasted_iota(jnp.int32, mo.shape, 0)
    mo[...] = jnp.where(row8 == 0, kept[0], jnp.where(row8 == 1, op[0], op[1]))
    mall[c] = mo[...]

    barrier = pltpu.get_barrier_semaphore()
    source = jnp.where(c == 0, up, down)
    greet = [partner, (source, 2 * x), (source, 2 * x + 1)]
    greet += [(s, 2 * t + h) for t in toward for h in range(2)]
    for dev in greet:
        pl.semaphore_signal(barrier, inc=1, device_id=dev, device_id_type=pl.DeviceIdType.MESH)
    pl.semaphore_wait(barrier, len(greet))

    give_left = [
        remote(left.at[:, chips[i]], lraw.at[own2, pl.ds(i * rc, rc)], s_pl.at[i], r_pl.at[i], partner)
        for i in range(4)
    ]
    give_right = remote(right, rown.at[own2], s_pr.at[0], r_pr.at[0], partner)
    give_meta = remote(mo, mall.at[c], s_pm.at[0], r_pm.at[0], partner)
    zdev = [(down, 2 * x), (up, 2 * x + 1)]
    give_z = [
        remote(right.at[t], rnbr.at[2 * c + t], s_zr.at[i, t], r_zr.at[c, t], zdev[i]) for t in range(2) for i in range(2)
    ]
    give_zm = [remote(mo, mz.at[c], s_zm.at[i], r_zm.at[c], zdev[i]) for i in range(2)]
    for copy in [give_meta, *give_left, give_right, *give_z, *give_zm]:
        copy.start()

    sign = jnp.where(c == 0, 0.5, -0.5).astype(F32)

    def scale_left(cc):
        for t in range(2):
            which = mall[cc, pl.ds(1 + t, 1), :]
            diag = jnp.where(which == 0, 1.0, jnp.where(which == 1, -0.25, 0.0))
            diag = jnp.where(which == 3, sign, jnp.where(which == 4, -sign, diag))
            flip = jnp.where(which == 2, 0.5, 0.0)
            outer = jnp.where(which == 0, 1.0, jnp.where(which == 1, 0.25, 0.0))
            outer = jnp.where(which >= 3, sign, outer)
            mat = lraw[2 * cc + t].astype(F32)
            lin[2 * cc + t, :, :size] = (mat * diag).astype(BF16)
            lin[2 * cc + t, :, size:] = (mat * flip).astype(BF16)
            lout[2 * cc + t] = (mat * outer).astype(BF16)

    for copy in loads[:5]:
        copy.wait()
    scale_left(c)
    give_meta.wait_recv()
    for copy in give_left:
        copy.wait_recv()
    scale_left(1 - c)
    give_right.wait_recv()
    for copy in loads[5:]:
        copy.wait()

    column = lax.broadcasted_iota(jnp.int32, (size, size), 1)

    def give_far(g, v, sgn):
        return remote(sb.at[g, v, 0], ry.at[g, v], s_d2.at[g, v], r_ry.at[g, v], (s, 2 * toward[sgn] + c))

    def give_near(g, v, sgn, h):
        return remote(
            sb.at[g, v, 1, pl.ds(h * rd, rd)], rx.at[1 - sgn, c, g, v], s_dir.at[g, v, h], r_rx.at[1 - sgn, c, g, v],
            (s, 2 * toward[1 - sgn] + h),
        )

    def give_relay(g, v, sgn, h):
        return remote(
            rs.at[g, v, pl.ds(h * rd, rd)], rx.at[sgn, c, g, v], s_rel.at[g, v, h], r_rx.at[sgn, c, g, v],
            (s, 2 * toward[sgn] + h),
        )

    def give_chip(g, v):
        return remote(po.at[g, v], loc.at[c, g, v], s_po.at[g, v], r_po.at[g, v], partner)

    def compute(g, limit):
        lmat, pmat, rmat = (lin, pin, rown) if g == 0 else (lout, pout, rnbr)

        def step(jj, carry):
            for sgn in range(2):
                v = jj + 2 * sgn
                vec = pmat[v].reshape(-1, size)
                total = jnp.zeros((size, size), F32)
                for t in range(4):
                    lifted = jnp.dot(lmat[t], vec, preferred_element_type=F32).astype(BF16)
                    total += nt_dot(lifted, rmat[t])
                total = jnp.where(column < limit, total, 0.0)
                parts = [total[i * rc : (i + 1) * rc] for i in range(4)]
                sb[g, v, 0] = parts[0].astype(BF16)
                sb[g, v, 1] = parts[2 - sgn].astype(BF16)
                give_far(g, v, sgn).start()
                for h in range(2):
                    give_near(g, v, sgn, h).start()
                kf[g, v] = parts[1 + sgn]
                first, second = parts[3][:rd], parts[3][rd:]
                loc[c, g, v] = jnp.where(c == 0, first, second)
                po[g, v] = jnp.where(c == 0, second, first)
                give_chip(g, v).start()
            return carry

        lax.fori_loop(0, nvec // 2, step, 0)

    def relay(g):
        def step(jj, carry):
            for sgn in range(2):
                v = jj + 2 * sgn
                give_far(g, v, sgn).wait_recv()
                rs[g, v] = (kf[g, v] + ry[g, v].astype(F32)).astype(BF16)
                for h in range(2):
                    give_relay(g, v, sgn, h).start()
            return carry

        lax.fori_loop(0, nvec // 2, step, 0)

    row = lax.broadcasted_iota(jnp.int32, (rd, size), 0) + k * rd
    mine = mo[pl.ds(0, 1), :]

    def give_out(v, p):
        return local(ob.at[v, p], out.at[v, p], s_out.at[v, p])

    def arrival(side, cc, g, v):
        return remote(rx.at[side, cc, g, v], rx.at[side, cc, g, v], s_po.at[g, v], r_rx.at[side, cc, g, v], partner)

    def finish(g):
        def step(v, carry):
            give_chip(g, v).wait_recv()
            for cc in range(2):
                p = 3 * cc if g else 1 + cc
                for side in range(2):
                    arrival(side, cc, g, v).wait_recv()
                total = loc[cc, g, v] + rx[0, cc, g, v].astype(F32) + rx[1, cc, g, v].astype(F32)
                ob[v, p] = jnp.where(row < mine, total, 0.0)
                give_out(v, p).start()
            return carry

        lax.fori_loop(0, nvec, step, 0)

    compute(0, mine)
    relay(0)
    for cc in range(2):
        for t in range(2):
            remote(right.at[t], rnbr.at[2 * cc + t], s_zr.at[0, t], r_zr.at[cc, t], partner).wait_recv()
        remote(mo, mz.at[cc], s_zm.at[0], r_zm.at[cc], partner).wait_recv()
    edge = jnp.where(c == 0, sectors - 1, 0)
    compute(1, jnp.where(s == edge, 0, mz[0, pl.ds(0, 1), :]))
    finish(0)
    relay(1)
    finish(1)

    for copy in [give_meta, *give_left, give_right, *give_z, *give_zm]:
        copy.wait_send()

    def drain(v, carry):
        for g in range(2):
            give_far(g, v, 0).wait_send()
            for h in range(2):
                give_near(g, v, 0, h).wait_send()
                give_relay(g, v, 0, h).wait_send()
            give_chip(g, v).wait_send()
        for p in range(4):
            give_out(v, p).wait()
        return carry

    lax.fori_loop(0, nvec, drain, 0)


def shards(psi, left, right, op, kept):
    nvec, _, phys, size, _ = psi.shape
    rc, rd = size // NX, size // NX // 2
    sectors = lax.axis_size("sector")
    dma = pltpu.SemaphoreType.DMA
    vmem = pltpu.VMEM
    scratch = [
        vmem((nvec, 2, size, size), BF16),
        vmem((nvec, size, size), BF16),
        vmem((4, size, size), BF16),
        vmem((4, size, 2 * size), BF16),
        vmem((4, size, size), BF16),
        vmem((4, size, size), BF16),
        vmem((4, size, size), BF16),
        vmem((8, size), jnp.int32),
        vmem((2, 8, size), jnp.int32),
        vmem((2, 8, size), jnp.int32),
        vmem((2, nvec, 2, rc, size), BF16),
        vmem((2, nvec, rc, size), F32),
        vmem((2, nvec, rc, size), BF16),
        vmem((2, nvec, rc, size), BF16),
        vmem((2, 2, 2, nvec, rd, size), BF16),
        vmem((2, nvec, rd, size), F32),
        vmem((2, 2, nvec, rd, size), F32),
        vmem((nvec, phys, rd, size), F32),
        dma((8,)),
        dma((4,)), dma((4,)), dma((1,)), dma((1,)), dma((1,)), dma((1,)),
        dma((2, 2)), dma((2, 2)), dma((2,)), dma((2,)),
        dma((2, nvec)), dma((2, nvec)), dma((2, nvec, 2)), dma((2, nvec, 2)), dma((2, 2, 2, nvec)),
        dma((2, nvec)), dma((2, nvec)), dma((nvec, phys)),
    ]
    anyspace = pl.BlockSpec(memory_space=pl.ANY)
    smem = pl.BlockSpec(memory_space=pltpu.SMEM)
    result = pl.pallas_call(
        functools.partial(kernel, sectors),
        out_shape=jax.ShapeDtypeStruct((nvec, phys, rd, size), F32),
        in_specs=[anyspace, anyspace, anyspace, smem, smem],
        out_specs=anyspace,
        scratch_shapes=scratch,
        compiler_params=pltpu.CompilerParams(collective_id=0, has_side_effects=True),
    )(
        psi.reshape(nvec, phys, size, size),
        left.reshape(2, NX, rc, size),
        right.reshape(2, size, size),
        op,
        kept,
    )
    return result[:, None]


def solution(mesh):
    in_specs = (
        P(None, "sector", None, None, None),
        P("term", "sector", None, None),
        P("term", "sector", None, None),
        P("term"),
        P("sector"),
    )
    out_specs = P(None, "sector", None, "term", None)
    return jax.shard_map(shards, mesh=mesh, in_specs=in_specs, out_specs=out_specs, check_vma=False)
```

time: 161 us -> 36.6 us (0.23)
  waiting for transfers between devices: 93.7 us -> 0 us
  Pallas kernels: 0 us -> 33.9 us
  matrix products: 18.9 us -> 0 us
  starting transfers between devices: 14.4 us -> 0 us
  between operations: 14.2 us -> 0.66 us
  local copies, waits for them, and re-layouts: 12.7 us -> 1.88 us
  other arithmetic: 5.66 us -> 0 us
    unnamed x2 -> x0, waiting for transfers between devices: 52 us -> none
    ppermute x4 -> x0, waiting for transfers between devices: 41.7 us -> none  [the longest x2 23.8 us: padded_2(): lax.ppermute(lax.slice_in_dim(block, 0, width, axis=dim), axis, backward)]
    pallas_call x0 -> x1, Pallas kernels: none -> 33.9 us  [shards(): pl.pallas_call(functools.partial(kernel, sectors), out_shape=jax.ShapeDty...]
    dot_general x4 -> x0, matrix products: 18.9 us -> none  [the longest x1 14.2 us: combine_terms(): jnp.einsum('uci,ufimy->fcmy', term_factor, mapped_vectors, precision=lax....]
    ppermute x4 -> x0, starting transfers between devices: 14.4 us -> none  [the longest x2 11.8 us: padded_2(): lax.ppermute(lax.slice_in_dim(block, block.shape[dim] - width, None, axis...]
    unnamed x10 -> x1, local copies, waits for them, and re-layouts: 8.78 us -> 1.88 us
    unnamed x1 -> x0, other arithmetic: 5.65 us -> none
    another operation x2 -> x0, local copies, waits for them, and re-layouts: 1.76 us -> none  [the longest x1 1.62 us: shards(): jnp.stack([right_side[:, 0], right_side[:, 3]], 0)]
  transfers between devices with their start and end apart: 5 -> 0, of which waited for: 5 -> 0; matrix products, arithmetic and copies ran while one was open for 1% -> 0% of each run, Pallas kernels for 0% -> 0%
where the time goes in v1:
time: 36.6 us; the launch traced here: 36.4 us
  Pallas kernels  33.9 us (93%)
  local copies, waits for them, and re-layouts  1.88 us (5%)
  between operations  0.66 us (2%)
    pallas_call x1, Pallas kernels, shards(): pl.pallas_call(functools.partial(kernel, sectors), out_shape=jax.ShapeDty...  33.9 us
    unnamed x1, local copies, waits for them, and re-layouts  1.88 us

profile of v1, /device:TPU:1, one launch (start us, length us, event | category | flops | bytes accessed | tf_op | source)
XLA Modules:
  0.0 36.4 jit_solution(17095530300444964603)
XLA Ops:
  0.7 33.9 %shard_map.55 = f32[4,4,32,256]{3,2,1,0:T(8,128)} custom-call(bf16[4,4,256,256]{3,2,1,0:T(8,128)(2,1)} %bitcast.6, bf16[2,4,64,256]{3,2,1,0:T(8,128)(2,1)} %bitcast.8, bf16[2,256,256]{2,1,0:T(8,128)(2,1)} %bitcast.9, s32[2]{0:T(128)} %op.1, s32[1]{0:T(128)S(6)} %copy.8.kept), custom_call_target="tpu_custom_call" | custom-call | tf_op jit(solution)/shard_map/pallas_call | solution.py:255
  34.5 1.9 %copy.9 = f32[4,1,4,32,256]{4,3,2,1,0:T(8,128)} copy(f32[4,1,4,32,256]{4,3,2,1,0:T(8,128)} %bitcast.7) | data formatting | bytes 1048576

commit v2 on v1

v2 whole, which is shorter than its diff:
```python
import functools

import jax
import jax.numpy as jnp
from jax import lax
from jax.experimental import pallas as pl
from jax.experimental.pallas import tpu as pltpu
from jax.sharding import PartitionSpec as P

F32 = jnp.float32
BF16 = jnp.bfloat16
NX = 4


def local(src, dst, sem):
    return pltpu.make_async_copy(src, dst, sem)


def remote(src, dst, send, recv, dev):
    return pltpu.make_async_remote_copy(
        src_ref=src, dst_ref=dst, send_sem=send, recv_sem=recv, device_id=dev, device_id_type=pl.DeviceIdType.MESH
    )


def nt_dot(a, b):
    return lax.dot_general(a, b, (((1,), (1,)), ((), ())), preferred_element_type=F32)


def kernel(
    sectors, psi, left, right, op, kept, out,
    pin, pout, lraw, lin, lout, rown, rnbr, lf, mo, mall, mz,
    fb0, nb0, kf0, rs0, ry0, rx0, po0, loc0, fb1, nb1, kf1, rs1, ry1, rx1, po1, loc1, ob,
    s_load, s_pl, r_pl, s_pr, r_pr, s_pm, r_pm, s_zr, r_zr, s_zm, r_zm,
    s_d2, r_ry, s_dir, s_rel, r_rx, s_po, r_po, s_out,
):
    nvec, _, size, _ = psi.shape
    rc, rd = size // NX, size // NX // 2
    s = lax.axis_index("sector")
    k = lax.axis_index("term")
    x, c = lax.div(k, 2), lax.rem(k, 2)
    up = lax.rem(s + 1, sectors)
    down = lax.rem(s + sectors - 1, sectors)
    plus = lax.rem(x + 1, NX)
    minus = lax.rem(x + NX - 1, NX)
    partner = (s, 2 * x + 1 - c)
    own2 = pl.ds(2 * c, 2)
    chips = [lax.rem(x + off, NX) for off in (2, 1, 3, 0)]
    toward = [plus, minus]

    loads = [local(left.at[:, chips[i]], lraw.at[own2, pl.ds(i * rc, rc)], s_load.at[i]) for i in range(4)]
    loads += [
        local(right, rown.at[own2], s_load.at[4]),
        local(psi.at[:, 1 + c], pin.at[:, 0], s_load.at[5]),
        local(psi.at[:, 2 - c], pin.at[:, 1], s_load.at[6]),
        local(psi.at[:, 3 * c], pout, s_load.at[7]),
    ]
    for copy in loads:
        copy.start()
    row8 = lax.broadcasted_iota(jnp.int32, mo.shape, 0)
    mo[...] = jnp.where(row8 == 0, kept[0], jnp.where(row8 == 1, op[0], op[1]))
    mall[c] = mo[...]

    barrier = pltpu.get_barrier_semaphore()
    source = jnp.where(c == 0, up, down)
    greet = [partner, (source, 2 * x), (source, 2 * x + 1)]
    greet += [(s, 2 * t + h) for t in toward for h in range(2)]
    for dev in greet:
        pl.semaphore_signal(barrier, inc=1, device_id=dev, device_id_type=pl.DeviceIdType.MESH)
    pl.semaphore_wait(barrier, len(greet))

    give_left = [
        remote(left.at[:, chips[i]], lraw.at[own2, pl.ds(i * rc, rc)], s_pl.at[i], r_pl.at[i], partner)
        for i in range(4)
    ]
    give_right = remote(right, rown.at[own2], s_pr.at[0], r_pr.at[0], partner)
    give_meta = remote(mo, mall.at[c], s_pm.at[0], r_pm.at[0], partner)
    zdev = [(down, 2 * x), (up, 2 * x + 1)]
    half = size // 2
    give_z = [
        remote(
            right.at[:, pl.ds(h * half, half)], rnbr.at[own2, pl.ds(h * half, half)], s_zr.at[i, h], r_zr.at[c, h], zdev[i]
        )
        for h in range(2) for i in range(2)
    ]
    give_zm = [remote(mo, mz.at[c], s_zm.at[i], r_zm.at[c], zdev[i]) for i in range(2)]
    for copy in [give_meta, *give_left, give_right, *give_zm, *give_z]:
        copy.start()

    sign = jnp.where(c == 0, 0.5, -0.5).astype(F32)

    def scale_left(cc):
        for t in range(2):
            which = mall[cc, pl.ds(1 + t, 1), :]
            diag = jnp.where(which == 0, 1.0, jnp.where(which == 1, -0.25, 0.0))
            diag = jnp.where(which == 3, sign, jnp.where(which == 4, -sign, diag))
            flip = jnp.where(which == 2, 0.5, 0.0)
            outer = jnp.where(which == 0, 1.0, jnp.where(which == 1, 0.25, 0.0))
            outer = jnp.where(which >= 3, sign, outer)
            mat = lraw[2 * cc + t].astype(F32)
            lin[2 * cc + t, :, :size] = (mat * diag).astype(BF16)
            lin[2 * cc + t, :, size:] = (mat * flip).astype(BF16)
            lout[2 * cc + t] = (mat * outer).astype(BF16)

    for copy in loads[:5]:
        copy.wait()
    scale_left(c)
    give_meta.wait_recv()
    for copy in give_left:
        copy.wait_recv()
    scale_left(1 - c)
    give_right.wait_recv()
    for copy in loads[5:]:
        copy.wait()

    fb, nb, kf, rs, ry = (fb0, fb1), (nb0, nb1), (kf0, kf1), (rs0, rs1), (ry0, ry1)
    rx, po, loc = (rx0, rx1), (po0, po1), (loc0, loc1)

    def give_far(g, a, sgn):
        return remote(fb[g].at[a, sgn], ry[g].at[a, sgn], s_d2.at[g, a, sgn], r_ry.at[g, a, sgn], (s, 2 * toward[sgn] + c))

    def give_near(g, a, sgn, h):
        return remote(
            nb[g].at[a, sgn, h], rx[g].at[1 - sgn, c, a, sgn], s_dir.at[g, a, sgn, h], r_rx.at[g, 1 - sgn, c, a, sgn],
            (s, 2 * toward[1 - sgn] + h),
        )

    def give_relay(g, a, sgn, h):
        return remote(
            rs[g].at[a, sgn, h], rx[g].at[sgn, c, a, sgn], s_rel.at[g, a, sgn, h], r_rx.at[g, sgn, c, a, sgn],
            (s, 2 * toward[sgn] + h),
        )

    def give_chip(g, a, sgn):
        return remote(po[g].at[a, sgn], loc[g].at[c, a, sgn], s_po.at[g, a, sgn], r_po.at[g, a, sgn], partner)

    def parts_of(total):
        return [total[i * rc : (i + 1) * rc].reshape(2, rd, -1) for i in range(4)]

    def inner(jj, carry):
        for sgn in range(2):
            v = jj + 2 * sgn
            vec = pin[v].reshape(-1, size)
            total = jnp.zeros((size, size), F32)
            for t in range(4):
                lifted = jnp.dot(lin[t], vec, preferred_element_type=F32).astype(BF16)
                total += nt_dot(lifted, rown[t])
            column = lax.broadcasted_iota(jnp.int32, total.shape, 1)
            parts = parts_of(jnp.where(column < mine, total, 0.0))
            fb0[jj, sgn] = parts[0].astype(BF16)
            give_far(0, jj, sgn).start()
            nb0[jj, sgn] = parts[2 - sgn].astype(BF16)
            for h in range(2):
                give_near(0, jj, sgn, h).start()
            kf0[jj, sgn] = parts[1 + sgn]
            loc0[c, jj, sgn] = jnp.where(c == 0, parts[3][0], parts[3][1])
            po0[jj, sgn] = jnp.where(c == 0, parts[3][1], parts[3][0])
            give_chip(0, jj, sgn).start()
        return carry

    def lift_outer(v, carry):
        for t in range(4):
            lf[v, t] = jnp.dot(lout[t], pout[v], preferred_element_type=F32).astype(BF16)
        return carry

    def outer(a, limit):
        for sgn in range(2):
            for jj in range(2):
                total = jnp.zeros((size, half), F32)
                for t in range(4):
                    total += nt_dot(lf[2 * sgn + jj, t], rnbr[t, pl.ds(a * half, half), :])
                column = lax.broadcasted_iota(jnp.int32, total.shape, 1) + a * half
                parts = parts_of(jnp.where(column < limit, total, 0.0))
                fb1[a, sgn, :, jj] = parts[0].astype(BF16)
                nb1[a, sgn, :, jj] = parts[2 - sgn].astype(BF16)
                kf1[a, sgn, :, jj] = parts[1 + sgn]
                loc1[c, a, sgn, jj] = jnp.where(c == 0, parts[3][0], parts[3][1])
                po1[a, sgn, jj] = jnp.where(c == 0, parts[3][1], parts[3][0])
            give_far(1, a, sgn).start()
        for sgn in range(2):
            for h in range(2):
                give_near(1, a, sgn, h).start()
            give_chip(1, a, sgn).start()

    def relay(g, a):
        for sgn in range(2):
            give_far(g, a, sgn).wait_recv()
            rs[g][a, sgn] = (kf[g][a, sgn] + ry[g][a, sgn].astype(F32)).astype(BF16)
            for h in range(2):
                give_relay(g, a, sgn, h).start()

    row = lax.broadcasted_iota(jnp.int32, (rd, size), 0) + k * rd
    mine = mo[pl.ds(0, 1), :]

    def give_out(v, p):
        return local(ob.at[v, p], out.at[v, p], s_out.at[v, p])

    def arrival(g, side, cc, a, sgn):
        piece = rx[g].at[side, cc, a, sgn]
        return remote(piece, piece, s_po.at[g, a, sgn], r_rx.at[g, side, cc, a, sgn], partner)

    def gathered(g, cc, a, sgn):
        for side in range(2):
            arrival(g, side, cc, a, sgn).wait_recv()
        total = loc[g][cc, a, sgn]
        for side in range(2):
            total += rx[g][side, cc, a, sgn].astype(F32)
        return total

    def finish_inner(jj, carry):
        for sgn in range(2):
            v = jj + 2 * sgn
            give_chip(0, jj, sgn).wait_recv()
            for cc in range(2):
                ob[v, 1 + cc] = jnp.where(row < mine, gathered(0, cc, jj, sgn), 0.0)
                give_out(v, 1 + cc).start()
        return carry

    def finish_outer(a):
        for sgn in range(2):
            give_chip(1, a, sgn).wait_recv()
            for cc in range(2):
                total = gathered(1, cc, a, sgn)
                for jj in range(2):
                    v = 2 * sgn + jj
                    ob[v, 3 * cc, :, pl.ds(a * half, half)] = jnp.where(row[:, :half] < mine[:, :half], total[jj], 0.0)
                    if a == 1:
                        give_out(v, 3 * cc).start()

    def wait_z(h):
        for cc in range(2):
            remote(
                right.at[:, pl.ds(h * half, half)], rnbr.at[pl.ds(2 * cc, 2), pl.ds(h * half, half)],
                s_zr.at[0, h], r_zr.at[cc, h], partner,
            ).wait_recv()

    lax.fori_loop(0, nvec // 2, inner, 0)
    lax.fori_loop(0, nvec, lift_outer, 0)
    relay(0, 0)
    for cc in range(2):
        remote(mo, mz.at[cc], s_zm.at[0], r_zm.at[cc], partner).wait_recv()
    edge = jnp.where(c == 0, sectors - 1, 0)
    limit = jnp.where(s == edge, 0, mz[0, pl.ds(0, 1), :])[:, :half]
    wait_z(0)
    outer(0, limit)
    relay(0, 1)
    wait_z(1)
    outer(1, limit)
    relay(1, 0)
    lax.fori_loop(0, nvec // 2, finish_inner, 0)
    relay(1, 1)
    finish_outer(0)
    finish_outer(1)

    for copy in [give_meta, *give_left, give_right, *give_z, *give_zm]:
        copy.wait_send()

    def drain(a, carry):
        for sgn in range(2):
            for g in range(2):
                give_far(g, a, sgn).wait_send()
                for h in range(2):
                    give_near(g, a, sgn, h).wait_send()
                    give_relay(g, a, sgn, h).wait_send()
                give_chip(g, a, sgn).wait_send()
            for p in range(4):
                give_out(a + 2 * sgn, p).wait()
        return carry

    lax.fori_loop(0, nvec // 2, drain, 0)


def shards(psi, left, right, op, kept):
    nvec, _, phys, size, _ = psi.shape
    rc, rd = size // NX, size // NX // 2
    sectors = lax.axis_size("sector")
    dma = pltpu.SemaphoreType.DMA
    vmem = pltpu.VMEM
    scratch = [
        vmem((nvec, 2, size, size), BF16),
        vmem((nvec, size, size), BF16),
        vmem((4, size, size), BF16),
        vmem((4, size, 2 * size), BF16),
        vmem((4, size, size), BF16),
        vmem((4, size, size), BF16),
        vmem((4, size, size), BF16),
        vmem((nvec, 4, size, size), BF16),
        vmem((8, size), jnp.int32),
        vmem((2, 8, size), jnp.int32),
        vmem((2, 8, size), jnp.int32),
    ]
    for piece in ((rd, size), (2, rd, size // 2)):
        scratch += [
            vmem((2, 2, 2, *piece), BF16),
            vmem((2, 2, 2, *piece), BF16),
            vmem((2, 2, 2, *piece), F32),
            vmem((2, 2, 2, *piece), BF16),
            vmem((2, 2, 2, *piece), BF16),
            vmem((2, 2, 2, 2, *piece), BF16),
            vmem((2, 2, *piece), F32),
            vmem((2, 2, 2, *piece), F32),
        ]
    scratch += [
        vmem((nvec, phys, rd, size), F32),
        dma((8,)),
        dma((4,)), dma((4,)), dma((1,)), dma((1,)), dma((1,)), dma((1,)),
        dma((2, 2)), dma((2, 2)), dma((2,)), dma((2,)),
        dma((2, 2, 2)), dma((2, 2, 2)), dma((2, 2, 2, 2)), dma((2, 2, 2, 2)), dma((2, 2, 2, 2, 2)),
        dma((2, 2, 2)), dma((2, 2, 2)), dma((nvec, phys)),
    ]
    anyspace = pl.BlockSpec(memory_space=pl.ANY)
    smem = pl.BlockSpec(memory_space=pltpu.SMEM)
    result = pl.pallas_call(
        functools.partial(kernel, sectors),
        out_shape=pltpu.VMEM((nvec, phys, rd, size), F32),
        in_specs=[anyspace, anyspace, anyspace, smem, smem],
        out_specs=anyspace,
        scratch_shapes=scratch,
        compiler_params=pltpu.CompilerParams(collective_id=0, has_side_effects=True, vmem_limit_bytes=56 * 2**20),
    )(
        psi.reshape(nvec, phys, size, size),
        left.reshape(2, NX, rc, size),
        right.reshape(2, size, size),
        op,
        kept,
    )
    return result[:, None]


def solution(mesh):
    in_specs = (
        P(None, "sector", None, None, None),
        P("term", "sector", None, None),
        P("term", "sector", None, None),
        P("term"),
        P("sector"),
    )
    out_specs = P(None, "sector", None, "term", None)
    return jax.shard_map(shards, mesh=mesh, in_specs=in_specs, out_specs=out_specs, check_vma=False)
```

time: 36.6 us -> 34.2 us (0.934)
  Pallas kernels: 33.9 us -> 32.7 us
  local copies, waits for them, and re-layouts: 1.88 us -> 0.8 us
    pallas_call x1, Pallas kernels: 33.9 us -> 32.7 us  [shards(): pl.pallas_call(functools.partial(kernel, sectors), out_shape=pltpu.VMEM((...]
    unnamed x1, local copies, waits for them, and re-layouts: 1.88 us -> 0.8 us
where the time goes in v2:
time: 34.2 us; the launch traced here: 34.1 us
  Pallas kernels  32.7 us (96%)
  local copies, waits for them, and re-layouts  0.8 us (2%)
  between operations  0.66 us (2%)
    pallas_call x1, Pallas kernels, shards(): pl.pallas_call(functools.partial(kernel, sectors), out_shape=pltpu.VMEM((...  32.7 us
    unnamed x1, local copies, waits for them, and re-layouts  0.8 us

profile of v2, /device:TPU:1, one launch (start us, length us, event | category | flops | bytes accessed | tf_op | source)
XLA Modules:
  0.0 34.1 jit_solution(8433684352633403412)
XLA Ops:
  0.7 32.7 %shard_map.55 = f32[4,4,32,256]{3,2,1,0:T(8,128)S(1)} custom-call(bf16[4,4,256,256]{3,2,1,0:T(8,128)(2,1)} %bitcast.7, bf16[2,4,64,256]{3,2,1,0:T(8,128)(2,1)} %bitcast.8, bf16[2,256,256]{2,1,0:T(8,128)(2,1)} %bitcast.9, s32[2]{0:T(128)} %op.1, s32[1]{0:T(128)S(6)} %copy.9.kept), custom_call_target="tpu_custom_call" | custom-call | tf_op jit(solution)/shard_map/pallas_call | solution.py:312
  33.3 0.8 %copy.8 = f32[4,1,4,32,256]{4,3,2,1,0:T(8,128)} copy(f32[4,1,4,32,256]{4,3,2,1,0:T(8,128)S(1)} %bitcast.6) | data formatting | bytes 1048576

commit v3 on v2

--- a/solution.py
+++ b/solution.py
@@ -29,9 +29,9 @@
 def kernel(
     sectors, psi, left, right, op, kept, out,
     pin, pout, lraw, lin, lout, rown, rnbr, lf, mo, mall, mz,
-    fb0, nb0, kf0, rs0, ry0, rx0, po0, loc0, fb1, nb1, kf1, rs1, ry1, rx1, po1, loc1, ob,
+    fb0, nb0, kf0, rs0, ry0, rx0, po0, loc0, fb1, nb1, kf1, rs1, ry1, rx1, po1, loc1,
     s_load, s_pl, r_pl, s_pr, r_pr, s_pm, r_pm, s_zr, r_zr, s_zm, r_zm,
-    s_d2, r_ry, s_dir, s_rel, r_rx, s_po, r_po, s_out,
+    s_d2, r_ry, s_dir, s_rel, r_rx, s_po, r_po,
 ):
     nvec, _, size, _ = psi.shape
     rc, rd = size // NX, size // NX // 2
@@ -191,9 +191,6 @@
     row = lax.broadcasted_iota(jnp.int32, (rd, size), 0) + k * rd
     mine = mo[pl.ds(0, 1), :]
 
-    def give_out(v, p):
-        return local(ob.at[v, p], out.at[v, p], s_out.at[v, p])
-
     def arrival(g, side, cc, a, sgn):
         piece = rx[g].at[side, cc, a, sgn]
         return remote(piece, piece, s_po.at[g, a, sgn], r_rx.at[g, side, cc, a, sgn], partner)
@@ -211,8 +208,7 @@
             v = jj + 2 * sgn
             give_chip(0, jj, sgn).wait_recv()
             for cc in range(2):
-                ob[v, 1 + cc] = jnp.where(row < mine, gathered(0, cc, jj, sgn), 0.0)
-                give_out(v, 1 + cc).start()
+                out[v, 1 + cc] = jnp.where(row < mine, gathered(0, cc, jj, sgn), 0.0)
         return carry
 
     def finish_outer(a):
@@ -222,9 +218,7 @@
                 total = gathered(1, cc, a, sgn)
                 for jj in range(2):
                     v = 2 * sgn + jj
-                    ob[v, 3 * cc, :, pl.ds(a * half, half)] = jnp.where(row[:, :half] < mine[:, :half], total[jj], 0.0)
-                    if a == 1:
-                        give_out(v, 3 * cc).start()
+                    out[v, 3 * cc, :, pl.ds(a * half, half)] = jnp.where(row[:, :half] < mine[:, :half], total[jj], 0.0)
 
     def wait_z(h):
         for cc in range(2):
@@ -262,8 +256,6 @@
                     give_near(g, a, sgn, h).wait_send()
                     give_relay(g, a, sgn, h).wait_send()
                 give_chip(g, a, sgn).wait_send()
-            for p in range(4):
-                give_out(a + 2 * sgn, p).wait()
         return carry
 
     lax.fori_loop(0, nvec // 2, drain, 0)
@@ -300,12 +292,11 @@
             vmem((2, 2, 2, *piece), F32),
         ]
     scratch += [
-        vmem((nvec, phys, rd, size), F32),
         dma((8,)),
         dma((4,)), dma((4,)), dma((1,)), dma((1,)), dma((1,)), dma((1,)),
         dma((2, 2)), dma((2, 2)), dma((2,)), dma((2,)),
         dma((2, 2, 2)), dma((2, 2, 2)), dma((2, 2, 2, 2)), dma((2, 2, 2, 2)), dma((2, 2, 2, 2, 2)),
-        dma((2, 2, 2)), dma((2, 2, 2)), dma((nvec, phys)),
+        dma((2, 2, 2)), dma((2, 2, 2)),
     ]
     anyspace = pl.BlockSpec(memory_space=pl.ANY)
     smem = pl.BlockSpec(memory_space=pltpu.SMEM)
@@ -313,7 +304,7 @@
         functools.partial(kernel, sectors),
         out_shape=pltpu.VMEM((nvec, phys, rd, size), F32),
         in_specs=[anyspace, anyspace, anyspace, smem, smem],
-        out_specs=anyspace,
+        out_specs=pl.BlockSpec(memory_space=pltpu.VMEM),
         scratch_shapes=scratch,
         compiler_params=pltpu.CompilerParams(collective_id=0, has_side_effects=True, vmem_limit_bytes=56 * 2**20),
     )(

time: 34.2 us -> 33.7 us (0.985)
  Pallas kernels: 32.7 us -> 32.1 us
    pallas_call x1, Pallas kernels: 32.7 us -> 32.1 us  [shards(): pl.pallas_call(functools.partial(kernel, sectors), out_shape=pltpu.VMEM((...]
where the time goes in v3:
time: 33.7 us; the launch traced here: 33.5 us
  Pallas kernels  32.1 us (95%)
  local copies, waits for them, and re-layouts  0.8 us (2%)
  between operations  0.66 us (2%)
    pallas_call x1, Pallas kernels, shards(): pl.pallas_call(functools.partial(kernel, sectors), out_shape=pltpu.VMEM((...  32.1 us
    unnamed x1, local copies, waits for them, and re-layouts  0.8 us

profile of v3, /device:TPU:1, one launch (start us, length us, event | category | flops | bytes accessed | tf_op | source)
XLA Modules:
  0.0 33.5 jit_solution(10841775259237805004)
XLA Ops:
  0.7 32.1 %shard_map.55 = f32[4,4,32,256]{3,2,1,0:T(8,128)S(1)} custom-call(bf16[4,4,256,256]{3,2,1,0:T(8,128)(2,1)} %bitcast.7, bf16[2,4,64,256]{3,2,1,0:T(8,128)(2,1)} %bitcast.8, bf16[2,256,256]{2,1,0:T(8,128)(2,1)} %bitcast.9, s32[2]{0:T(128)} %op.1, s32[1]{0:T(128)S(6)} %copy.9.kept), custom_call_target="tpu_custom_call" | custom-call | tf_op jit(solution)/shard_map/pallas_call | solution.py:303
  32.8 0.8 %copy.8 = f32[4,1,4,32,256]{4,3,2,1,0:T(8,128)} copy(f32[4,1,4,32,256]{4,3,2,1,0:T(8,128)S(1)} %bitcast.6) | data formatting | bytes 1048576

commit v4 on v3

--- a/solution.py
+++ b/solution.py
@@ -176,10 +176,12 @@
                 loc1[c, a, sgn, jj] = jnp.where(c == 0, parts[3][0], parts[3][1])
                 po1[a, sgn, jj] = jnp.where(c == 0, parts[3][1], parts[3][0])
             give_far(1, a, sgn).start()
+            give_chip(1, a, sgn).start()
+
+    def nears(a):
         for sgn in range(2):
             for h in range(2):
                 give_near(1, a, sgn, h).start()
-            give_chip(1, a, sgn).start()
 
     def relay(g, a):
         for sgn in range(2):
@@ -240,6 +242,8 @@
     wait_z(1)
     outer(1, limit)
     relay(1, 0)
+    nears(0)
+    nears(1)
     lax.fori_loop(0, nvec // 2, finish_inner, 0)
     relay(1, 1)
     finish_outer(0)

time: 33.7 us -> 33 us (0.979)
  Pallas kernels: 32.1 us -> 31.5 us
    pallas_call x1, Pallas kernels: 32.1 us -> 31.5 us  [shards(): pl.pallas_call(functools.partial(kernel, sectors), out_shape=pltpu.VMEM((...]
where the time goes in v4:
time: 33 us; the launch traced here: 32.9 us
  Pallas kernels  31.5 us (95%)
  local copies, waits for them, and re-layouts  0.8 us (2%)
  between operations  0.66 us (2%)
    pallas_call x1, Pallas kernels, shards(): pl.pallas_call(functools.partial(kernel, sectors), out_shape=pltpu.VMEM((...  31.5 us
    unnamed x1, local copies, waits for them, and re-layouts  0.8 us

profile of v4, /device:TPU:1, one launch (start us, length us, event | category | flops | bytes accessed | tf_op | source)
XLA Modules:
  0.0 32.9 jit_solution(10600188574850818826)
XLA Ops:
  0.7 31.5 %shard_map.55 = f32[4,4,32,256]{3,2,1,0:T(8,128)S(1)} custom-call(bf16[4,4,256,256]{3,2,1,0:T(8,128)(2,1)} %bitcast.7, bf16[2,4,64,256]{3,2,1,0:T(8,128)(2,1)} %bitcast.8, bf16[2,256,256]{2,1,0:T(8,128)(2,1)} %bitcast.9, s32[2]{0:T(128)} %op.1, s32[1]{0:T(128)S(6)} %copy.9.kept), custom_call_target="tpu_custom_call" | custom-call | tf_op jit(solution)/shard_map/pallas_call | solution.py:307
  32.1 0.8 %copy.8 = f32[4,1,4,32,256]{4,3,2,1,0:T(8,128)} copy(f32[4,1,4,32,256]{4,3,2,1,0:T(8,128)S(1)} %bitcast.6) | data formatting | bytes 1048576

commit v5 on v4

--- a/solution.py
+++ b/solution.py
@@ -244,8 +244,8 @@
     relay(1, 0)
     nears(0)
     nears(1)
+    relay(1, 1)
     lax.fori_loop(0, nvec // 2, finish_inner, 0)
-    relay(1, 1)
     finish_outer(0)
     finish_outer(1)
 

time: 33 us -> 33 us (level)
  no operation moved by 1% of the time
where the time goes in v5:
time: 33 us; the launch traced here: 32.9 us
  Pallas kernels  31.5 us (95%)
  local copies, waits for them, and re-layouts  0.8 us (2%)
  between operations  0.66 us (2%)
    pallas_call x1, Pallas kernels, shards(): pl.pallas_call(functools.partial(kernel, sectors), out_shape=pltpu.VMEM((...  31.5 us
    unnamed x1, local copies, waits for them, and re-layouts  0.8 us

profile of v5, /device:TPU:1, one launch (start us, length us, event | category | flops | bytes accessed | tf_op | source)
XLA Modules:
  0.0 32.9 jit_solution(16100889151432507850)
XLA Ops:
  0.7 31.5 %shard_map.55 = f32[4,4,32,256]{3,2,1,0:T(8,128)S(1)} custom-call(bf16[4,4,256,256]{3,2,1,0:T(8,128)(2,1)} %bitcast.7, bf16[2,4,64,256]{3,2,1,0:T(8,128)(2,1)} %bitcast.8, bf16[2,256,256]{2,1,0:T(8,128)(2,1)} %bitcast.9, s32[2]{0:T(128)} %op.1, s32[1]{0:T(128)S(6)} %copy.9.kept), custom_call_target="tpu_custom_call" | custom-call | tf_op jit(solution)/shard_map/pallas_call | solution.py:307
  32.1 0.8 %copy.8 = f32[4,1,4,32,256]{4,3,2,1,0:T(8,128)} copy(f32[4,1,4,32,256]{4,3,2,1,0:T(8,128)S(1)} %bitcast.6) | data formatting | bytes 1048576

commit v6 on v5

--- a/solution.py
+++ b/solution.py
@@ -236,9 +236,9 @@
         remote(mo, mz.at[cc], s_zm.at[0], r_zm.at[cc], partner).wait_recv()
     edge = jnp.where(c == 0, sectors - 1, 0)
     limit = jnp.where(s == edge, 0, mz[0, pl.ds(0, 1), :])[:, :half]
+    relay(0, 1)
     wait_z(0)
     outer(0, limit)
-    relay(0, 1)
     wait_z(1)
     outer(1, limit)
     relay(1, 0)

time: 33 us -> 34.3 us (1.039)
  Pallas kernels: 31.5 us -> 32.7 us
    pallas_call x1, Pallas kernels: 31.5 us -> 32.7 us  [shards(): pl.pallas_call(functools.partial(kernel, sectors), out_shape=pltpu.VMEM((...]
where the time goes in v6:
time: 34.3 us; the launch traced here: 34.2 us
  Pallas kernels  32.7 us (95%)
  local copies, waits for them, and re-layouts  0.8 us (2%)
  between operations  0.66 us (2%)
    pallas_call x1, Pallas kernels, shards(): pl.pallas_call(functools.partial(kernel, sectors), out_shape=pltpu.VMEM((...  32.7 us
    unnamed x1, local copies, waits for them, and re-layouts  0.8 us

profile of v6, /device:TPU:1, one launch (start us, length us, event | category | flops | bytes accessed | tf_op | source)
XLA Modules:
  0.0 34.2 jit_solution(5840598738202687080)
XLA Ops:
  0.7 32.7 %shard_map.55 = f32[4,4,32,256]{3,2,1,0:T(8,128)S(1)} custom-call(bf16[4,4,256,256]{3,2,1,0:T(8,128)(2,1)} %bitcast.7, bf16[2,4,64,256]{3,2,1,0:T(8,128)(2,1)} %bitcast.8, bf16[2,256,256]{2,1,0:T(8,128)(2,1)} %bitcast.9, s32[2]{0:T(128)} %op.1, s32[1]{0:T(128)S(6)} %copy.9.kept), custom_call_target="tpu_custom_call" | custom-call | tf_op jit(solution)/shard_map/pallas_call | solution.py:307
  33.4 0.8 %copy.8 = f32[4,1,4,32,256]{4,3,2,1,0:T(8,128)} copy(f32[4,1,4,32,256]{4,3,2,1,0:T(8,128)S(1)} %bitcast.6) | data formatting | bytes 1048576
